TPU v7x, 32 devices: a whole 2x2x4 slice. The times are simulated.
32 devices in a mesh: win: 2 (over x), row: 16 (over z, y, core).
Axes of the slice: x: 2, y: 2, z: 4, core: 2. Of those that a mesh axis runs over, the one named last changes fastest.
Arguments:
- mask_field: float32 [2, 4096, 128], P(None, ('win', 'row')), parts along dimension 1, may hold values from -6 to 6
- target: int32 [4096, 128], P(('win', 'row')), parts along dimension 0, may hold values 0 or 1
- kernel_taps: float32 [24, 2, 128, 128], replicated, may hold values from -0.046875 to 0.046875
- kernel_radii: int32 [24], replicated, may hold values from 16 to 64, as said below
- kernel_group: int32 [24], replicated, may hold values from 0 to 2, as said below
- kernel_weight: float32 [24], replicated, may hold values from 0.1 to 1
Outputs:
- resist: float32 [3, 4096, 128], P(None, ('win', 'row')), parts along dimension 1
- gradient: float32 [2, 4096, 128], P(None, ('win', 'row')), parts along dimension 1
There are 2 independent parts, one for each index of `win`. A program takes and returns all parts, laid end to end along the dimension named above; an argument that names none is the same for every part. Nothing has to cross between parts.
Inputs may be any that keep to these rules, and one draw needn't show every extreme that they name: `kernel_radii`: every radius lies in 16 to 64; some kernel has radius exactly 64 and some exactly 16. `kernel_group`: every one of the 3 process conditions holds at least one kernel.
All inputs are finite; a program needn't handle non-finite values. No bound on the sum of `target` on one device may be relied on, other than what follows from the above.
Results may differ from a plain program's by a relative error of at most 0.0003.
Values sent between devices are 32-bit elements; how exact they have to be, the bound alone decides.
A program may use at most 128 MiB of HBM per device.

v0:
```python
import numpy as np

import jax
import jax.numpy as jnp
from jax import lax
from jax.experimental import pallas as pl
from jax.experimental.pallas import tpu as pltpu
from jax.sharding import PartitionSpec as P

RMAX = 64
GROUPS = 3
STEEPNESS = 1.0
THRESHOLD = 2.0


def split_np(table):
    high = table.astype(jnp.bfloat16)
    low = (table - high.astype(np.float64)).astype(jnp.bfloat16)
    return high, low


def angles(points, grid):
    freqs = np.arange(grid // 2, dtype=np.int64)
    turns = (points.astype(np.int64)[:, None] * (2 * freqs[None, :] + 1)) % (2 * grid)
    return turns.astype(np.float64) * (np.pi / grid)


def tables(rows, cols):
    taps = 2 * RMAX
    grid_rows, grid_cols = rows + taps, cols + taps
    tap = np.arange(taps) - RMAX
    own, ext, col = np.arange(rows), np.arange(grid_rows) - RMAX, np.arange(cols)

    def right(points, grid):
        ang = angles(points, grid)
        high, low = split_np(np.concatenate([np.cos(ang), np.sin(ang)], 1))
        return np.stack([np.concatenate([high, high], 0), np.concatenate([low, low], 0)])

    def left(points, grid, deep):
        ang = angles(points, grid).T
        high, low = split_np(np.concatenate([np.cos(ang), np.sin(ang)], 0))
        if deep:
            high, low = np.concatenate([high, high], 1), np.concatenate([low, low], 1)
        return np.concatenate([high, low], 0)

    def back_left(points, grid):
        ang = angles(points, grid)
        high, low = split_np(np.concatenate([np.cos(ang), np.sin(ang)], 1) / grid)
        return np.concatenate([high, low], 0)

    def back_right(points, grid):
        ang = angles(points, grid).T
        high, low = split_np(np.concatenate([np.cos(ang), np.sin(ang)], 0) / grid)
        return np.concatenate([high, low], 1)

    return (
        right(tap, grid_cols),
        right(col, grid_cols),
        left(tap, grid_rows, True),
        left(own, grid_rows, True),
        left(ext, grid_rows, False),
        back_left(own, grid_rows),
        back_left(ext, grid_rows),
        back_right(col, grid_cols),
    )


def dot(a, b):
    return lax.dot_general(a, b, (((1,), (0,)), ((), ())), preferred_element_type=jnp.float32)


def split(value):
    high = value.astype(jnp.bfloat16)
    low = (value - high.astype(jnp.float32)).astype(jnp.bfloat16)
    return high, low


def col_transform(pair, table):
    high, low = split(pair)
    data = jnp.concatenate([high, low], axis=1)
    return dot(data, table[0]) + dot(data, table[1])


def fold(value):
    half = value.shape[0] // 2
    return value[:half] + value[half:]


def row_transform(value, table):
    high, low = split(value)
    return fold(dot(table, jnp.concatenate([high, low], axis=0)))


def row_transform_wide(value, table):
    high, low = split(value)
    return fold(dot(table, high)) + dot(table[: table.shape[0] // 2], low)


def quadrants(real, imag):
    g, f = real.shape[0] // 2, real.shape[1] // 2

    def parts(v):
        cp, cq, sp, sq = v[:g, :f], v[:g, f:], v[g:, :f], v[g:, f:]
        return cp - sq, sp + cq, cp + sq, sp - cq

    e1r, e2r, e3r, e4r = parts(real)
    e1i, e2i, e3i, e4i = parts(imag)
    return (
        (e1r + e2i, e1i - e2r),
        (e1r - e2i, e1i + e2r),
        (e3r + e4i, e3i - e4r),
        (e3r - e4i, e3i + e4r),
    )


def inverse(quads, row_table, col_table):
    (pr, pi), (mr, mi), (qr, qi), (nr, ni) = quads
    sr, dr, tr, er = pr + mr, pr - mr, qr + nr, qr - nr
    si, di, ti, ei = pi + mi, pi - mi, qi + ni, qi - ni

    def stack(a, b, c, d):
        return jnp.concatenate(
            [jnp.concatenate([a, b], axis=1), jnp.concatenate([c, d], axis=1)], axis=0
        )

    real = stack(sr + tr, ei - di, -di - ei, tr - sr)
    imag = stack(si + ti, dr - er, dr + er, ti - si)
    half = jnp.concatenate(
        [row_transform_wide(real, row_table), row_transform_wide(imag, row_table)], axis=0
    )
    high, low = split(half)
    both = fold(dot(jnp.concatenate([high, low], axis=0), col_table))
    width = both.shape[1] // 2
    return both[:, :width] + both[:, width:]


def body(
    radii_ref,
    group_ref,
    weight_ref,
    taps_ref,
    mask_ref,
    target_ref,
    tap_col,
    own_col,
    tap_row,
    own_row,
    ext_row,
    back_own,
    back_ext,
    back_col,
    resist_ref,
    adjoint_ref,
    spec,
    fields,
    mask_spec,
    total,
):
    kernels = taps_ref.shape[0]
    taps = taps_ref.shape[2]
    rows, cols = target_ref.shape

    def spectrum(k, carry):
        radius = radii_ref[k]
        a = lax.broadcasted_iota(jnp.int32, (taps, taps), 0) - RMAX
        b = lax.broadcasted_iota(jnp.int32, (taps, taps), 1) - RMAX
        inside = (a >= -radius) & (a < radius) & (b >= -radius) & (b < radius)
        pair = jnp.concatenate(
            [jnp.where(inside, taps_ref[k, 0], 0.0), jnp.where(inside, taps_ref[k, 1], 0.0)], axis=0
        )
        half = col_transform(pair, tap_col)
        real = row_transform(half[:taps], tap_row[...])
        imag = row_transform(half[taps:], tap_row[...])
        for q, (re, im) in enumerate(quadrants(real, imag)):
            spec[k, 2 * q] = re
            spec[k, 2 * q + 1] = im
        return carry

    lax.fori_loop(0, kernels, spectrum, 0)

    ext = mask_ref.shape[1]
    half = col_transform(jnp.concatenate([mask_ref[0], mask_ref[1]], axis=0), own_col)
    real = row_transform_wide(half[:ext], ext_row[...])
    imag = row_transform_wide(half[ext:], ext_row[...])
    for q, (re, im) in enumerate(quadrants(real, imag)):
        mask_spec[2 * q] = re
        mask_spec[2 * q + 1] = im

    resist_ref[...] = jnp.zeros_like(resist_ref)

    def mixed(k, g):
        return jnp.where(group_ref[k] == g, weight_ref[k], 0.0)

    def forward(k, carry):
        quads = []
        for q in range(4):
            xr, xi = spec[k, 2 * q], spec[k, 2 * q + 1]
            mr, mi = mask_spec[2 * q], mask_spec[2 * q + 1]
            quads.append((xr * mr - xi * mi, xr * mi + xi * mr))
        field = inverse(quads, back_own[...], back_col[...])
        fields[k] = field
        power = field[:rows] * field[:rows] + field[rows:] * field[rows:]
        for g in range(GROUPS):
            resist_ref[g] += mixed(k, g) * power
        return carry

    lax.fori_loop(0, kernels, forward, 0)

    target = target_ref[...].astype(jnp.float32)
    slopes = []
    for g in range(GROUPS):
        resist = jax.nn.sigmoid(STEEPNESS * (resist_ref[g] - THRESHOLD))
        resist_ref[g] = resist
        total[g] = 2.0 * (resist - target) * resist * (1.0 - resist) * STEEPNESS
    for q in range(8):
        mask_spec[q] = jnp.zeros_like(mask_spec[q])

    def backward(k, carry):
        factor = sum(2.0 * mixed(k, g) * total[g] for g in range(GROUPS))
        field = fields[k]
        cot = jnp.concatenate([factor * field[:rows], factor * field[rows:]], axis=0)
        half = col_transform(cot, own_col)
        real = row_transform(half[:rows], own_row[...])
        imag = row_transform(half[rows:], own_row[...])
        for q, (wr, wi) in enumerate(quadrants(real, imag)):
            xr, xi = spec[k, 2 * q], spec[k, 2 * q + 1]
            mask_spec[2 * q] += xr * wr + xi * wi
            mask_spec[2 * q + 1] += xr * wi - xi * wr
        return carry

    lax.fori_loop(0, kernels, backward, 0)
    quads = [(mask_spec[2 * q], mask_spec[2 * q + 1]) for q in range(4)]
    adjoint = inverse(quads, back_ext[...], back_col[...])
    adjoint_ref[0] = adjoint[:ext]
    adjoint_ref[1] = adjoint[ext:]


def padded(cells, width):
    count = lax.axis_size("row")
    head, tail = cells[:, :width], cells[:, cells.shape[1] - width :]
    above = lax.ppermute(tail, "row", [(i, i + 1) for i in range(count - 1)])
    below = lax.ppermute(head, "row", [(i + 1, i) for i in range(count - 1)])
    return jnp.concatenate([above, cells, below], axis=1)


def on_device(mask_field, target, kernel_taps, kernel_radii, kernel_group, kernel_weight):
    rows, cols = target.shape
    kernels = kernel_taps.shape[0]
    grid_rows, grid_cols = rows + 2 * RMAX, cols + 2 * RMAX
    consts = [jnp.asarray(t) for t in tables(rows, cols)]
    extended = padded(mask_field, RMAX)
    vmem = pl.BlockSpec(memory_space=pltpu.VMEM)
    smem = pl.BlockSpec(memory_space=pltpu.SMEM)
    plane = (grid_rows // 2, grid_cols // 2)
    resist, adjoint = pl.pallas_call(
        body,
        out_shape=(
            jax.ShapeDtypeStruct((GROUPS, rows, cols), jnp.float32),
            jax.ShapeDtypeStruct((2, grid_rows, cols), jnp.float32),
        ),
        in_specs=[smem] * 3 + [vmem] * (3 + len(consts)),
        out_specs=(vmem, vmem),
        scratch_shapes=[
            pltpu.VMEM((kernels, 8) + plane, jnp.float32),
            pltpu.VMEM((kernels, 2 * rows, cols), jnp.float32),
            pltpu.VMEM((8,) + plane, jnp.float32),
            pltpu.VMEM((GROUPS, rows, cols), jnp.float32),
        ],
        compiler_params=pltpu.CompilerParams(vmem_limit_bytes=48 * 1024 * 1024),
        name="litho",
    )(kernel_radii, kernel_group, kernel_weight, kernel_taps, extended, target, *consts)
    own = adjoint[:, RMAX : RMAX + rows]
    count = lax.axis_size("row")
    below = lax.ppermute(adjoint[:, :RMAX], "row", [(i + 1, i) for i in range(count - 1)])
    above = lax.ppermute(adjoint[:, RMAX + rows :], "row", [(i, i + 1) for i in range(count - 1)])
    rest = rows - RMAX
    gradient = (
        own
        + jnp.pad(above, ((0, 0), (0, rest), (0, 0)))
        + jnp.pad(below, ((0, 0), (rest, 0), (0, 0)))
    )
    return resist, gradient


def solution(mesh):
    in_specs = (P(None, ("win", "row"), None), P(("win", "row"), None), P(), P(), P(), P())
    out_specs = (P(None, ("win", "row"), None), P(None, ("win", "row"), None))
    return jax.shard_map(
        on_device, mesh=mesh, in_specs=in_specs, out_specs=out_specs, check_vma=False
    )
```

profile of v0, /device:TPU:1, one launch (start us, length us, event | category | flops | bytes accessed | tf_op | source)
XLA Modules:
  0.0 77.1 jit_solution(16371387078258338804)
XLA Ops:
  0.6 0.9 %fusion.1 = (f32[2,64,128]{2,1,0:T(8,128)S(1)}, f32[2,64,128]{2,1,0:T(8,128)S(1)}) fusion(f32[2,128,128]{2,1,0:T(8,128)} %param.14), kind=kLoop, calls=%fused_computation.3 | loop fusion | bytes 262144 | tf_op jit(solution)/shard_map/slice | solution.py:240
  1.5 4.5 %collective-permute-start = (f32[2,64,128]{2,1,0:T(8,128)S(1)}, f32[2,64,128]{2,1,0:T(8,128)S(1)}, u32[]{:S(2)}, u32[]{:S(2)}) collective-permute-start(f32[2,64,128]{2,1,0:T(8,128)S(1)} %get-tuple-element.8), channel_id=1, source_target_pairs={{0,1},{1,2},{2,3},{3,4},{4,5},{5,6},{6,7},{7,8},{8,9},{9,10},{10,1... | collective-permute-start | bytes 196616 | tf_op jit(solution)/shard_map/ppermute | solution.py:241
  6.1 1.9 %collective-permute-start.1 = (f32[2,64,128]{2,1,0:T(8,128)S(1)}, f32[2,64,128]{2,1,0:T(8,128)S(1)}, u32[]{:S(2)}, u32[]{:S(2)}) collective-permute-start(f32[2,64,128]{2,1,0:T(8,128)S(1)} %get-tuple-element.9), channel_id=1, source_target_pairs={{1,0},{2,1},{3,2},{4,3},{5,4},{6,5},{7,6},{8,7},{9,8},{10,9},{11,1... | collective-permute-start | bytes 196616 | tf_op jit(solution)/shard_map/ppermute | solution.py:242
  8.0 3.6 %collective-permute-done.1 = f32[2,64,128]{2,1,0:T(8,128)S(1)} collective-permute-done((f32[2,64,128]{2,1,0:T(8,128)S(1)}, f32[2,64,128]{2,1,0:T(8,128)S(1)}, u32[]{:S(2)}, u32[]{:S(2)}) %collective-permute-start.1) | collective-permute-done | bytes 65568 | tf_op jit(solution)/shard_map/ppermute | solution.py:242
  11.6 0.9 %pad_maximum_fusion.mask_ref = f32[2,256,128]{2,1,0:T(8,128)S(1)} fusion(f32[2,64,128]{2,1,0:T(8,128)S(1)} %collective-permute-done.1, f32[2,128,128]{2,1,0:T(8,128)} %param.14, f32[2,64,128]{2,1,0:T(8,128)S(1)} %collective-permute-done), kind=kLoop, calls=%fused_computation | loop fusion | flops 131072 | bytes 524288 | tf_op jit(solution)/shard_map/concatenate | solution.py:243
  12.6 0.0 copy-start
  12.6 1.9 %copy-done = f32[24,2,128,128]{3,2,1,0:T(8,128)S(1)} copy-done((f32[24,2,128,128]{3,2,1,0:T(8,128)S(1)}, f32[24,2,128,128]{3,2,1,0:T(8,128)}, u32[]{:S(2)}) %copy-start) | copy-done | bytes 3145752
  14.5 0.9 %copy-done.1 = bf16[512,256]{1,0:T(8,128)(2,1)S(1)} copy-done((bf16[512,256]{1,0:T(8,128)(2,1)S(1)}, bf16[512,256]{1,0:T(8,128)(2,1)}, u32[]{:S(2)}) %copy-start.1) | copy-done | bytes 262168
  15.4 0.9 %copy-done.2 = bf16[512,256]{1,0:T(8,128)(2,1)S(1)} copy-done((bf16[512,256]{1,0:T(8,128)(2,1)S(1)}, bf16[512,256]{1,0:T(8,128)(2,1)}, u32[]{:S(2)}) %copy-start.2) | copy-done | bytes 262168
  16.4 0.9 %copy-done.3 = bf16[512,256]{1,0:T(8,128)(2,1)S(1)} copy-done((bf16[512,256]{1,0:T(8,128)(2,1)S(1)}, bf16[512,256]{1,0:T(8,128)(2,1)}, u32[]{:S(2)}) %copy-start.3) | copy-done | bytes 262168
  17.3 0.9 %copy-done.4 = bf16[512,256]{1,0:T(8,128)(2,1)S(1)} copy-done((bf16[512,256]{1,0:T(8,128)(2,1)S(1)}, bf16[512,256]{1,0:T(8,128)(2,1)}, u32[]{:S(2)}) %copy-start.4) | copy-done | bytes 262168
  18.3 0.9 %copy-done.5 = bf16[2,256,256]{2,1,0:T(8,128)(2,1)S(1)} copy-done((bf16[2,256,256]{2,1,0:T(8,128)(2,1)S(1)}, bf16[2,256,256]{2,1,0:T(8,128)(2,1)}, u32[]{:S(2)}) %copy-start.5) | copy-done | bytes 262168
  19.2 0.9 %copy-done.6 = bf16[2,256,256]{2,1,0:T(8,128)(2,1)S(1)} copy-done((bf16[2,256,256]{2,1,0:T(8,128)(2,1)S(1)}, bf16[2,256,256]{2,1,0:T(8,128)(2,1)}, u32[]{:S(2)}) %copy-start.6) | copy-done | bytes 262168
  20.2 0.9 %copy-done.7 = bf16[256,256]{1,0:T(8,128)(2,1)S(1)} copy-done((bf16[256,256]{1,0:T(8,128)(2,1)S(1)}, bf16[256,256]{1,0:T(8,128)(2,1)}, u32[]{:S(2)}) %copy-start.7) | copy-done | bytes 131096
  21.1 0.9 %copy-done.8 = bf16[256,256]{1,0:T(8,128)(2,1)S(1)} copy-done((bf16[256,256]{1,0:T(8,128)(2,1)S(1)}, bf16[256,256]{1,0:T(8,128)(2,1)}, u32[]{:S(2)}) %copy-start.8) | copy-done | bytes 131096
  22.0 0.8 %copy-done.9 = s32[128,128]{1,0:T(8,128)S(1)} copy-done((s32[128,128]{1,0:T(8,128)S(1)}, s32[128,128]{1,0:T(8,128)}, u32[]{:S(2)}) %copy-start.9) | copy-done | bytes 65560
  22.8 0.7 copy-done.10
  23.5 0.7 copy-done.11
  24.1 0.7 copy-done.12
  24.8 43.3 %litho.1 = (f32[3,128,128]{2,1,0:T(8,128)}, f32[2,256,128]{2,1,0:T(8,128)S(1)}) custom-call(s32[24]{0:T(128)S(1)} %copy-done.10, s32[24]{0:T(128)S(1)} %copy-done.11, f32[24]{0:T(128)S(1)} %copy-done.12, f32[24,2,128,128]{3,2,1,0:T(8,128)S(1)} %copy-done, f32[2,256,128]{2,1,0:T(8,128)S(1)} %pad_maximum_fusion.mask_ref, s32[128,128]{1,0:T(8,128)S(1)} %copy-done.9, ...), custom_call_target="tpu_custom_call" | custom-call | tf_op jit(solution)/shard_map/litho/pallas_call | solution.py:255
  68.1 1.9 %collective-permute-start.2 = (f32[2,64,128]{2,1,0:T(8,128)S(1)}, f32[2,64,128]{2,1,0:T(8,128)S(1)}, u32[]{:S(2)}, u32[]{:S(2)}) collective-permute-start(f32[2,64,128]{2,1,0:T(8,128)S(1)} %get-tuple-element.6), channel_id=1, source_target_pairs={{0,1},{1,2},{2,3},{3,4},{4,5},{5,6},{6,7},{7,8},{8,9},{9,10},{10,1... | collective-permute-start | bytes 196616 | tf_op jit(solution)/shard_map/ppermute | solution.py:275
  70.1 2.4 %collective-permute-start.3 = (f32[2,64,128]{2,1,0:T(8,128)S(1)}, f32[2,64,128]{2,1,0:T(8,128)S(1)}, u32[]{:S(2)}, u32[]{:S(2)}) collective-permute-start(f32[2,64,128]{2,1,0:T(8,128)S(1)} %get-tuple-element.7), channel_id=1, source_target_pairs={{1,0},{2,1},{3,2},{4,3},{5,4},{6,5},{7,6},{8,7},{9,8},{10,9},{11,1... | collective-permute-start | bytes 196616 | tf_op jit(solution)/shard_map/ppermute | solution.py:274
  72.5 3.9 %collective-permute-done.3 = f32[2,64,128]{2,1,0:T(8,128)S(1)} collective-permute-done((f32[2,64,128]{2,1,0:T(8,128)S(1)}, f32[2,64,128]{2,1,0:T(8,128)S(1)}, u32[]{:S(2)}, u32[]{:S(2)}) %collective-permute-start.3) | collective-permute-done | bytes 65568 | tf_op jit(solution)/shard_map/ppermute | solution.py:274
  76.4 0.7 pad_add_fusion
  (15 shorter events, 0.0 us)
Async XLA Ops:
  1.5 6.5 %collective-permute-start = (f32[2,64,128]{2,1,0:T(8,128)S(1)}, f32[2,64,128]{2,1,0:T(8,128)S(1)}, u32[]{:S(2)}, u32[]{:S(2)}) collective-permute-start(f32[2,64,128]{2,1,0:T(8,128)S(1)} %get-tuple-element.8), channel_id=1, source_target_pairs={{0,1},{1,2},{2,3},{3,4},{4,5},{5,6},{6,7},{7,8},{8,9},{9,10},{10,1... | collective-permute-start | bytes 196616 | tf_op jit(solution)/shard_map/ppermute | solution.py:241
  6.1 5.6 %collective-permute-start.1 = (f32[2,64,128]{2,1,0:T(8,128)S(1)}, f32[2,64,128]{2,1,0:T(8,128)S(1)}, u32[]{:S(2)}, u32[]{:S(2)}) collective-permute-start(f32[2,64,128]{2,1,0:T(8,128)S(1)} %get-tuple-element.9), channel_id=1, source_target_pairs={{1,0},{2,1},{3,2},{4,3},{5,4},{6,5},{7,6},{8,7},{9,8},{10,9},{11,1... | collective-permute-start | bytes 196616 | tf_op jit(solution)/shard_map/ppermute | solution.py:242
  12.6 1.9 %copy-start = (f32[24,2,128,128]{3,2,1,0:T(8,128)S(1)}, f32[24,2,128,128]{3,2,1,0:T(8,128)}, u32[]{:S(2)}) copy-start(f32[24,2,128,128]{3,2,1,0:T(8,128)} %taps_ref.1) | copy-start | bytes 9437188
  14.5 0.9 %copy-start.1 = (bf16[512,256]{1,0:T(8,128)(2,1)S(1)}, bf16[512,256]{1,0:T(8,128)(2,1)}, u32[]{:S(2)}) copy-start(bf16[512,256]{1,0:T(8,128)(2,1)} %constant.25.clone.back_ext) | copy-start | bytes 786436
  15.4 0.9 %copy-start.2 = (bf16[512,256]{1,0:T(8,128)(2,1)S(1)}, bf16[512,256]{1,0:T(8,128)(2,1)}, u32[]{:S(2)}) copy-start(bf16[512,256]{1,0:T(8,128)(2,1)} %constant.23.clone.ext_row) | copy-start | bytes 786436
  16.4 0.9 %copy-start.3 = (bf16[512,256]{1,0:T(8,128)(2,1)S(1)}, bf16[512,256]{1,0:T(8,128)(2,1)}, u32[]{:S(2)}) copy-start(bf16[512,256]{1,0:T(8,128)(2,1)} %constant.22.clone.own_row) | copy-start | bytes 786436
  17.3 0.9 %copy-start.4 = (bf16[512,256]{1,0:T(8,128)(2,1)S(1)}, bf16[512,256]{1,0:T(8,128)(2,1)}, u32[]{:S(2)}) copy-start(bf16[512,256]{1,0:T(8,128)(2,1)} %constant.21.clone.tap_row) | copy-start | bytes 786436
  18.3 0.9 %copy-start.5 = (bf16[2,256,256]{2,1,0:T(8,128)(2,1)S(1)}, bf16[2,256,256]{2,1,0:T(8,128)(2,1)}, u32[]{:S(2)}) copy-start(bf16[2,256,256]{2,1,0:T(8,128)(2,1)} %constant.20.clone.own_col) | copy-start | bytes 786436
  19.2 0.9 %copy-start.6 = (bf16[2,256,256]{2,1,0:T(8,128)(2,1)S(1)}, bf16[2,256,256]{2,1,0:T(8,128)(2,1)}, u32[]{:S(2)}) copy-start(bf16[2,256,256]{2,1,0:T(8,128)(2,1)} %constant.19.clone.tap_col) | copy-start | bytes 786436
  20.2 0.9 %copy-start.7 = (bf16[256,256]{1,0:T(8,128)(2,1)S(1)}, bf16[256,256]{1,0:T(8,128)(2,1)}, u32[]{:S(2)}) copy-start(bf16[256,256]{1,0:T(8,128)(2,1)} %constant.26.clone.back_col) | copy-start | bytes 393220
  21.1 0.9 %copy-start.8 = (bf16[256,256]{1,0:T(8,128)(2,1)S(1)}, bf16[256,256]{1,0:T(8,128)(2,1)}, u32[]{:S(2)}) copy-start(bf16[256,256]{1,0:T(8,128)(2,1)} %constant.24.clone.back_own) | copy-start | bytes 393220
  22.0 0.8 %copy-start.9 = (s32[128,128]{1,0:T(8,128)S(1)}, s32[128,128]{1,0:T(8,128)}, u32[]{:S(2)}) copy-start(s32[128,128]{1,0:T(8,128)} %target_ref.1) | copy-start | bytes 196612
  22.8 0.7 copy-start.10
  23.5 0.7 copy-start.11
  24.1 0.7 copy-start.12
  68.1 4.3 %collective-permute-start.2 = (f32[2,64,128]{2,1,0:T(8,128)S(1)}, f32[2,64,128]{2,1,0:T(8,128)S(1)}, u32[]{:S(2)}, u32[]{:S(2)}) collective-permute-start(f32[2,64,128]{2,1,0:T(8,128)S(1)} %get-tuple-element.6), channel_id=1, source_target_pairs={{0,1},{1,2},{2,3},{3,4},{4,5},{5,6},{6,7},{7,8},{8,9},{9,10},{10,1... | collective-permute-start | bytes 196616 | tf_op jit(solution)/shard_map/ppermute | solution.py:275
  70.1 6.4 %collective-permute-start.3 = (f32[2,64,128]{2,1,0:T(8,128)S(1)}, f32[2,64,128]{2,1,0:T(8,128)S(1)}, u32[]{:S(2)}, u32[]{:S(2)}) collective-permute-start(f32[2,64,128]{2,1,0:T(8,128)S(1)} %get-tuple-element.7), channel_id=1, source_target_pairs={{1,0},{2,1},{3,2},{4,3},{5,4},{6,5},{7,6},{8,7},{9,8},{10,9},{11,1... | collective-permute-start | bytes 196616 | tf_op jit(solution)/shard_map/ppermute | solution.py:274
where the time goes:
time: 77.9 us; the launch traced here: 77.1 us
  Pallas kernels  43.3 us (56%)
  local copies, waits for them, and re-layouts  13.1 us (17%)
  starting transfers between devices  10.8 us (14%)
  waiting for transfers between devices  7.6 us (10%)
  other arithmetic  1.6 us (2%)
    pallas_call x1, Pallas kernels, on_device(): pl.pallas_call(body, out_shape=(jax.ShapeDtypeStruct((GROUPS, rows, cols)...  43.3 us
    unnamed x26, local copies, waits for them, and re-layouts  12.2 us
    ppermute x1, starting transfers between devices, padded(): above = lax.ppermute(tail, 'row', [(i, i + 1) for i in range(count - 1)])  4.53 us
    ppermute x1, waiting for transfers between devices, on_device(): lax.ppermute(adjoint[:, :RMAX], 'row', [(i + 1, i) for i in range(count -...  3.95 us
    ppermute x1, waiting for transfers between devices, padded(): below = lax.ppermute(head, 'row', [(i + 1, i) for i in range(count - 1)])  3.65 us
    ppermute x1, starting transfers between devices, on_device(): lax.ppermute(adjoint[:, :RMAX], 'row', [(i + 1, i) for i in range(count -...  2.41 us
    ppermute x1, starting transfers between devices, padded(): below = lax.ppermute(head, 'row', [(i + 1, i) for i in range(count - 1)])  1.92 us
    ppermute x1, starting transfers between devices, on_device(): lax.ppermute(adjoint[:, RMAX + rows:], 'row', [(i, i + 1) for i in range(...  1.92 us
  transfers between devices with their start and end apart: 4, of which 2 were waited for; matrix products, arithmetic and copies ran while one was open for 0% of the time, Pallas kernels for 0%

commit v1 on v0

--- a/solution.py
+++ b/solution.py
@@ -11,6 +11,8 @@
 GROUPS = 3
 STEEPNESS = 1.0
 THRESHOLD = 2.0
+UNROLL = (1, 1, 1)
+MESH = pl.DeviceIdType.MESH
 
 
 def split_np(table):
@@ -25,11 +27,15 @@
     return turns.astype(np.float64) * (np.pi / grid)
 
 
+def tap_like(count):
+    return np.arange(count) - RMAX
+
+
 def tables(rows, cols):
     taps = 2 * RMAX
     grid_rows, grid_cols = rows + taps, cols + taps
     tap = np.arange(taps) - RMAX
-    own, ext, col = np.arange(rows), np.arange(grid_rows) - RMAX, np.arange(cols)
+    own, ext, col = tap_like(rows), np.arange(grid_rows) - 2 * RMAX, tap_like(cols)
 
     def right(points, grid):
         ang = angles(points, grid)
@@ -138,29 +144,125 @@
     radii_ref,
     group_ref,
     weight_ref,
-    taps_ref,
-    mask_ref,
-    target_ref,
-    tap_col,
-    own_col,
-    tap_row,
-    own_row,
-    ext_row,
-    back_own,
-    back_ext,
-    back_col,
-    resist_ref,
-    adjoint_ref,
-    spec,
-    fields,
-    mask_spec,
-    total,
+    taps_hbm,
+    mask_hbm,
+    target_hbm,
+    *refs,
 ):
-    kernels = taps_ref.shape[0]
-    taps = taps_ref.shape[2]
-    rows, cols = target_ref.shape
+    table_hbm, refs = refs[:8], refs[8:]
+    resist_ref, grad_ref = refs[:2]
+    spec, fields, acc, slopes, taps_ref, ext_ref, target_ref, adj, rims = refs[2:11]
+    table_ref, refs = refs[11:19], refs[19:]
+    tap_sem, load_sem, send_sem, recv_sem = refs
+    tap_col, own_col, tap_row, own_row, ext_row, back_own, back_ext, back_col = table_ref
+    kernels, _, taps, _ = taps_hbm.shape
+    rows, cols = target_hbm.shape
+    me, count = lax.axis_index("row"), lax.axis_size("row")
+    has_prev, has_next = me > 0, me < count - 1
+    prev_id = {"row": lax.rem(me + count - 1, count)}
+    next_id = {"row": lax.rem(me + 1, count)}
+
+    def load(src, dst, slot):
+        return pltpu.make_async_copy(src, dst, load_sem.at[slot])
+
+    def tap_load(k):
+        return pltpu.make_async_copy(taps_hbm.at[k], taps_ref.at[k], tap_sem.at[k])
+
+    loads = [load(src, dst, i) for i, (src, dst) in enumerate(zip(table_hbm, table_ref))]
+    load_mask = load(mask_hbm, ext_ref.at[:, pl.ds(RMAX, rows)], 8)
+    load_target = load(target_hbm, target_ref, 9)
+    loads[0].start()
+    loads[2].start()
+
+    def start_tap(k, carry):
+        tap_load(k).start()
+        return carry
+
+    lax.fori_loop(0, kernels, start_tap, 0)
+    load_mask.start()
+    load_target.start()
+    for i in (1, 3, 4, 5, 6, 7):
+        loads[i].start()
+
+    barrier = pltpu.get_barrier_semaphore()
+
+    @pl.when(has_prev)
+    def _():
+        pl.semaphore_signal(barrier, inc=1, device_id=prev_id, device_id_type=MESH)
+
+    @pl.when(has_next)
+    def _():
+        pl.semaphore_signal(barrier, inc=1, device_id=next_id, device_id_type=MESH)
+
+    pl.semaphore_wait(barrier, has_prev.astype(jnp.int32) + has_next.astype(jnp.int32))
+
+    def exchange(first, src_up, dst_up, src_down, dst_down):
+        down = pltpu.make_async_remote_copy(
+            src_ref=src_down,
+            dst_ref=dst_down,
+            send_sem=send_sem.at[first],
+            recv_sem=recv_sem.at[first],
+            device_id=next_id,
+            device_id_type=MESH,
+        )
+        up = pltpu.make_async_remote_copy(
+            src_ref=src_up,
+            dst_ref=dst_up,
+            send_sem=send_sem.at[first + 1],
+            recv_sem=recv_sem.at[first + 1],
+            device_id=prev_id,
+            device_id_type=MESH,
+        )
+        return up, down
+
+    def start_both(pair):
+        up, down = pair
+
+        @pl.when(has_next)
+        def _():
+            down.start()
+
+        @pl.when(has_prev)
+        def _():
+            up.start()
+
+    def wait_both(pair):
+        up, down = pair
+
+        @pl.when(has_prev)
+        def _():
+            up.wait_send()
+            down.wait_recv()
+
+        @pl.when(has_next)
+        def _():
+            down.wait_send()
+            up.wait_recv()
+
+    halo = exchange(
+        0,
+        mask_hbm.at[:, pl.ds(0, RMAX)],
+        ext_ref.at[:, pl.ds(RMAX + rows, RMAX)],
+        mask_hbm.at[:, pl.ds(rows - RMAX, RMAX)],
+        ext_ref.at[:, pl.ds(0, RMAX)],
+    )
+    start_both(halo)
+
+    @pl.when(jnp.logical_not(has_prev))
+    def _():
+        ext_ref[:, :RMAX] = jnp.zeros_like(ext_ref[:, :RMAX])
+        rims[0] = jnp.zeros_like(rims[0])
+
+    @pl.when(jnp.logical_not(has_next))
+    def _():
+        ext_ref[:, RMAX + rows :] = jnp.zeros_like(ext_ref[:, RMAX + rows :])
+        rims[1] = jnp.zeros_like(rims[1])
+
+    loads[0].wait()
+    loads[2].wait()
 
     def spectrum(k, carry):
+        tap_load(k).wait()
         radius = radii_ref[k]
         a = lax.broadcasted_iota(jnp.int32, (taps, taps), 0) - RMAX
         b = lax.broadcasted_iota(jnp.int32, (taps, taps), 1) - RMAX
@@ -176,15 +278,21 @@
             spec[k, 2 * q + 1] = im
         return carry
 
-    lax.fori_loop(0, kernels, spectrum, 0)
-
-    ext = mask_ref.shape[1]
-    half = col_transform(jnp.concatenate([mask_ref[0], mask_ref[1]], axis=0), own_col)
+    lax.fori_loop(0, kernels, spectrum, 0, unroll=UNROLL[0])
+
+    load_mask.wait()
+    load_target.wait()
+    for i in (1, 3, 4, 5, 6, 7):
+        loads[i].wait()
+    wait_both(halo)
+
+    ext = ext_ref.shape[1]
+    half = col_transform(jnp.concatenate([ext_ref[0], ext_ref[1]], axis=0), own_col)
     real = row_transform_wide(half[:ext], ext_row[...])
     imag = row_transform_wide(half[ext:], ext_row[...])
     for q, (re, im) in enumerate(quadrants(real, imag)):
-        mask_spec[2 * q] = re
-        mask_spec[2 * q + 1] = im
+        acc[2 * q] = re
+        acc[2 * q + 1] = im
 
     resist_ref[...] = jnp.zeros_like(resist_ref)
 
@@ -195,7 +303,7 @@
         quads = []
         for q in range(4):
             xr, xi = spec[k, 2 * q], spec[k, 2 * q + 1]
-            mr, mi = mask_spec[2 * q], mask_spec[2 * q + 1]
+            mr, mi = acc[2 * q], acc[2 * q + 1]
             quads.append((xr * mr - xi * mi, xr * mi + xi * mr))
         field = inverse(quads, back_own[...], back_col[...])
         fields[k] = field
@@ -204,19 +312,17 @@
             resist_ref[g] += mixed(k, g) * power
         return carry
 
-    lax.fori_loop(0, kernels, forward, 0)
+    lax.fori_loop(0, kernels, forward, 0, unroll=UNROLL[1])
 
     target = target_ref[...].astype(jnp.float32)
-    slopes = []
     for g in range(GROUPS):
         resist = jax.nn.sigmoid(STEEPNESS * (resist_ref[g] - THRESHOLD))
         resist_ref[g] = resist
-        total[g] = 2.0 * (resist - target) * resist * (1.0 - resist) * STEEPNESS
-    for q in range(8):
-        mask_spec[q] = jnp.zeros_like(mask_spec[q])
+        slopes[g] = 2.0 * (resist - target) * resist * (1.0 - resist) * STEEPNESS
+    acc[...] = jnp.zeros_like(acc)
 
     def backward(k, carry):
-        factor = sum(2.0 * mixed(k, g) * total[g] for g in range(GROUPS))
+        factor = sum(2.0 * mixed(k, g) * slopes[g] for g in range(GROUPS))
         field = fields[k]
         cot = jnp.concatenate([factor * field[:rows], factor * field[rows:]], axis=0)
         half = col_transform(cot, own_col)
@@ -224,62 +330,69 @@
         imag = row_transform(half[rows:], own_row[...])
         for q, (wr, wi) in enumerate(quadrants(real, imag)):
             xr, xi = spec[k, 2 * q], spec[k, 2 * q + 1]
-            mask_spec[2 * q] += xr * wr + xi * wi
-            mask_spec[2 * q + 1] += xr * wi - xi * wr
+            acc[2 * q] += xr * wr + xi * wi
+            acc[2 * q + 1] += xr * wi - xi * wr
         return carry
 
-    lax.fori_loop(0, kernels, backward, 0)
-    quads = [(mask_spec[2 * q], mask_spec[2 * q + 1]) for q in range(4)]
+    lax.fori_loop(0, kernels, backward, 0, unroll=UNROLL[2])
+    quads = [(acc[2 * q], acc[2 * q + 1]) for q in range(4)]
     adjoint = inverse(quads, back_ext[...], back_col[...])
-    adjoint_ref[0] = adjoint[:ext]
-    adjoint_ref[1] = adjoint[ext:]
-
-
-def padded(cells, width):
-    count = lax.axis_size("row")
-    head, tail = cells[:, :width], cells[:, cells.shape[1] - width :]
-    above = lax.ppermute(tail, "row", [(i, i + 1) for i in range(count - 1)])
-    below = lax.ppermute(head, "row", [(i + 1, i) for i in range(count - 1)])
-    return jnp.concatenate([above, cells, below], axis=1)
+    adj[0] = adjoint[:ext]
+    adj[1] = adjoint[ext:]
+    back = exchange(
+        2,
+        adj.at[:, pl.ds(0, RMAX)],
+        rims.at[1],
+        adj.at[:, pl.ds(RMAX + rows, RMAX)],
+        rims.at[0],
+    )
+    start_both(back)
+    grad_ref[...] = adj[:, RMAX : RMAX + rows]
+    wait_both(back)
+    grad_ref[:, :RMAX] += rims[0]
+    grad_ref[:, rows - RMAX :] += rims[1]
 
 
 def on_device(mask_field, target, kernel_taps, kernel_radii, kernel_group, kernel_weight):
     rows, cols = target.shape
-    kernels = kernel_taps.shape[0]
-    grid_rows, grid_cols = rows + 2 * RMAX, cols + 2 * RMAX
+    kernels, _, taps, _ = kernel_taps.shape
+    grid_rows, grid_cols = rows + taps, cols + taps
     consts = [jnp.asarray(t) for t in tables(rows, cols)]
-    extended = padded(mask_field, RMAX)
     vmem = pl.BlockSpec(memory_space=pltpu.VMEM)
     smem = pl.BlockSpec(memory_space=pltpu.SMEM)
+    hbm = pl.BlockSpec(memory_space=pltpu.HBM)
     plane = (grid_rows // 2, grid_cols // 2)
-    resist, adjoint = pl.pallas_call(
+    return pl.pallas_call(
         body,
         out_shape=(
             jax.ShapeDtypeStruct((GROUPS, rows, cols), jnp.float32),
-            jax.ShapeDtypeStruct((2, grid_rows, cols), jnp.float32),
+            jax.ShapeDtypeStruct((2, rows, cols), jnp.float32),
         ),
-        in_specs=[smem] * 3 + [vmem] * (3 + len(consts)),
+        in_specs=[smem] * 3 + [hbm] * (3 + len(consts)),
         out_specs=(vmem, vmem),
         scratch_shapes=[
             pltpu.VMEM((kernels, 8) + plane, jnp.float32),
             pltpu.VMEM((kernels, 2 * rows, cols), jnp.float32),
             pltpu.VMEM((8,) + plane, jnp.float32),
             pltpu.VMEM((GROUPS, rows, cols), jnp.float32),
+            pltpu.VMEM(kernel_taps.shape, jnp.float32),
+            pltpu.VMEM((2, grid_rows, cols), jnp.float32),
+            pltpu.VMEM((rows, cols), jnp.int32),
+            pltpu.VMEM((2, grid_rows, cols), jnp.float32),
+            pltpu.VMEM((2, 2, RMAX, cols), jnp.float32),
+        ]
+        + [pltpu.VMEM(t.shape, t.dtype) for t in consts]
+        + [
+            pltpu.SemaphoreType.DMA((kernels,)),
+            pltpu.SemaphoreType.DMA((10,)),
+            pltpu.SemaphoreType.DMA((4,)),
+            pltpu.SemaphoreType.DMA((4,)),
         ],
-        compiler_params=pltpu.CompilerParams(vmem_limit_bytes=48 * 1024 * 1024),
+        compiler_params=pltpu.CompilerParams(
+            vmem_limit_bytes=56 * 1024 * 1024, collective_id=0, has_side_effects=True
+        ),
         name="litho",
-    )(kernel_radii, kernel_group, kernel_weight, kernel_taps, extended, target, *consts)
-    own = adjoint[:, RMAX : RMAX + rows]
-    count = lax.axis_size("row")
-    below = lax.ppermute(adjoint[:, :RMAX], "row", [(i + 1, i) for i in range(count - 1)])
-    above = lax.ppermute(adjoint[:, RMAX + rows :], "row", [(i, i + 1) for i in range(count - 1)])
-    rest = rows - RMAX
-    gradient = (
-        own
-        + jnp.pad(above, ((0, 0), (0, rest), (0, 0)))
-        + jnp.pad(below, ((0, 0), (rest, 0), (0, 0)))
-    )
-    return resist, gradient
+    )(kernel_radii, kernel_group, kernel_weight, kernel_taps, mask_field, target, *consts)
 
 
 def solution(mesh):

time: 77.9 us -> 54.1 us (0.69)
  starting transfers between devices: 10.8 us -> 0 us
  local copies, waits for them, and re-layouts: 13.1 us -> 3.18 us
  waiting for transfers between devices: 7.6 us -> 0 us
  Pallas kernels: 43.3 us -> 50.1 us
  other arithmetic: 1.6 us -> 0 us
    ppermute x4 -> x0, starting transfers between devices: 10.8 us -> none  [the longest x1 4.53 us: padded(): above = lax.ppermute(tail, 'row', [(i, i + 1) for i in range(count - 1)])]
    unnamed x26 -> x2, local copies, waits for them, and re-layouts: 12.2 us -> 3.18 us
    ppermute x4 -> x0, waiting for transfers between devices: 7.6 us -> none  [the longest x1 3.95 us: on_device(): lax.ppermute(adjoint[:, :RMAX], 'row', [(i + 1, i) for i in range(count -...]
    pallas_call x1, Pallas kernels: 43.3 us -> 50.1 us  [on_device(): pl.pallas_call(body, out_shape=(jax.ShapeDtypeStruct((GROUPS, rows, cols)...]
    concatenate x1 -> x0, other arithmetic: 0.92 us -> none  [padded(): return jnp.concatenate([above, cells, below], axis=1)]
    slice x2 -> x0, local copies, waits for them, and re-layouts: 0.9 us -> none  [the longest x1 0.89 us: padded(): head, tail = (cells[:, :width], cells[:, cells.shape[1] - width:])]
  transfers between devices with their start and end apart: 4 -> 0, of which waited for: 2 -> 0; matrix products, arithmetic and copies ran while one was open for 0% -> 0% of each run, Pallas kernels for 0% -> 0%
where the time goes in v1:
time: 54.1 us; the launch traced here: 54 us
  Pallas kernels  50.1 us (93%)
  local copies, waits for them, and re-layouts  3.18 us (6%)
  between operations  0.64 us (1%)
    pallas_call x1, Pallas kernels, on_device(): pl.pallas_call(body, out_shape=(jax.ShapeDtypeStruct((GROUPS, rows, cols)...  50.1 us
    unnamed x2, local copies, waits for them, and re-layouts  3.18 us

profile of v1, /device:TPU:1, one launch (start us, length us, event | category | flops | bytes accessed | tf_op | source)
XLA Modules:
  0.0 54.0 jit_solution(5931298728716117231)
XLA Ops:
  0.6 50.1 %litho.1 = (f32[3,128,128]{2,1,0:T(8,128)}, f32[2,128,128]{2,1,0:T(8,128)}) custom-call(s32[24]{0:T(128)} %radii_ref.1, s32[24]{0:T(128)} %group_ref.1, f32[24]{0:T(128)} %weight_ref.1, f32[24,2,128,128]{3,2,1,0:T(8,128)} %taps_hbm.1, f32[2,128,128]{2,1,0:T(8,128)} %mask_hbm.1, s32[128,128]{1,0:T(8,128)} %target_hbm.1, ...), custom_call_target="tpu_custom_call" | custom-call | tf_op jit(solution)/shard_map/litho/pallas_call | solution.py:365
  50.8 1.6 %copy.18 = f32[3,128,128]{2,1,0:T(8,128)} copy(f32[3,128,128]{2,1,0:T(8,128)} %get-tuple-element.4) | data formatting | bytes 393216
  52.4 1.6 %copy.19 = f32[2,128,128]{2,1,0:T(8,128)} copy(f32[2,128,128]{2,1,0:T(8,128)} %get-tuple-element.5) | data formatting | bytes 262144

commit v2 on v1

--- a/solution.py
+++ b/solution.py
@@ -11,7 +11,7 @@
 GROUPS = 3
 STEEPNESS = 1.0
 THRESHOLD = 2.0
-UNROLL = (1, 1, 1)
+UNROLL = (4, 6, 6)
 MESH = pl.DeviceIdType.MESH
 
 
@@ -69,6 +69,10 @@
         back_left(ext, grid_rows),
         back_right(col, grid_cols),
     )
+
+
+def resist_of(intensity):
+    return jax.nn.sigmoid(STEEPNESS * (intensity - THRESHOLD))
 
 
 def dot(a, b):
@@ -150,9 +154,9 @@
     *refs,
 ):
     table_hbm, refs = refs[:8], refs[8:]
-    resist_ref, grad_ref = refs[:2]
-    spec, fields, acc, slopes, taps_ref, ext_ref, target_ref, adj, rims = refs[2:11]
-    table_ref, refs = refs[11:19], refs[19:]
+    power_ref, own_ref, rim_ref = refs[:3]
+    spec, fields, acc, slopes, taps_ref, ext_ref, target_ref, adj, rims = refs[3:12]
+    table_ref, refs = refs[12:20], refs[20:]
     tap_sem, load_sem, send_sem, recv_sem = refs
     tap_col, own_col, tap_row, own_row, ext_row, back_own, back_ext, back_col = table_ref
     kernels, _, taps, _ = taps_hbm.shape
@@ -294,7 +298,7 @@
         acc[2 * q] = re
         acc[2 * q + 1] = im
 
-    resist_ref[...] = jnp.zeros_like(resist_ref)
+    power_ref[...] = jnp.zeros_like(power_ref)
 
     def mixed(k, g):
         return jnp.where(group_ref[k] == g, weight_ref[k], 0.0)
@@ -309,15 +313,14 @@
         fields[k] = field
         power = field[:rows] * field[:rows] + field[rows:] * field[rows:]
         for g in range(GROUPS):
-            resist_ref[g] += mixed(k, g) * power
+            power_ref[g] += mixed(k, g) * power
         return carry
 
     lax.fori_loop(0, kernels, forward, 0, unroll=UNROLL[1])
 
     target = target_ref[...].astype(jnp.float32)
     for g in range(GROUPS):
-        resist = jax.nn.sigmoid(STEEPNESS * (resist_ref[g] - THRESHOLD))
-        resist_ref[g] = resist
+        resist = resist_of(power_ref[g])
         slopes[g] = 2.0 * (resist - target) * resist * (1.0 - resist) * STEEPNESS
     acc[...] = jnp.zeros_like(acc)
 
@@ -347,10 +350,17 @@
         rims.at[0],
     )
     start_both(back)
-    grad_ref[...] = adj[:, RMAX : RMAX + rows]
+    own_ref[...] = adj[:, RMAX : RMAX + rows]
+    if rows > 2 * RMAX:
+        rim_ref[...] = jnp.zeros_like(rim_ref)
     wait_both(back)
-    grad_ref[:, :RMAX] += rims[0]
-    grad_ref[:, rows - RMAX :] += rims[1]
+    rim_ref[:, :RMAX] = rims[0]
+    rim_ref[:, rows - RMAX :] = rims[1]
+
+
+def finish(power_ref, own_ref, rim_ref, resist_ref, grad_ref):
+    resist_ref[...] = resist_of(power_ref[...])
+    grad_ref[...] = own_ref[...] + rim_ref[...]
 
 
 def on_device(mask_field, target, kernel_taps, kernel_radii, kernel_group, kernel_weight):
@@ -362,14 +372,15 @@
     smem = pl.BlockSpec(memory_space=pltpu.SMEM)
     hbm = pl.BlockSpec(memory_space=pltpu.HBM)
     plane = (grid_rows // 2, grid_cols // 2)
-    return pl.pallas_call(
+    intensity, own, rim = pl.pallas_call(
         body,
         out_shape=(
             jax.ShapeDtypeStruct((GROUPS, rows, cols), jnp.float32),
             jax.ShapeDtypeStruct((2, rows, cols), jnp.float32),
+            jax.ShapeDtypeStruct((2, rows, cols), jnp.float32),
         ),
         in_specs=[smem] * 3 + [hbm] * (3 + len(consts)),
-        out_specs=(vmem, vmem),
+        out_specs=(vmem, vmem, vmem),
         scratch_shapes=[
             pltpu.VMEM((kernels, 8) + plane, jnp.float32),
             pltpu.VMEM((kernels, 2 * rows, cols), jnp.float32),
@@ -393,6 +404,16 @@
         ),
         name="litho",
     )(kernel_radii, kernel_group, kernel_weight, kernel_taps, mask_field, target, *consts)
+    return pl.pallas_call(
+        finish,
+        out_shape=(
+            jax.ShapeDtypeStruct((GROUPS, rows, cols), jnp.float32),
+            jax.ShapeDtypeStruct((2, rows, cols), jnp.float32),
+        ),
+        in_specs=[vmem] * 3,
+        out_specs=(vmem, vmem),
+        name="finish",
+    )(intensity, own, rim)
 
 
 def solution(mesh):

time: 54.1 us -> 44.4 us (0.82)
  Pallas kernels: 50.1 us -> 43.6 us
  local copies, waits for them, and re-layouts: 3.18 us -> 0 us
    pallas_call x1, Pallas kernels: 50.1 us -> 41.8 us  [on_device(): pl.pallas_call(body, out_shape=(jax.ShapeDtypeStruct((GROUPS, rows, cols)...]
    unnamed x2 -> x0, local copies, waits for them, and re-layouts: 3.18 us -> none
    pallas_call x0 -> x1, Pallas kernels: none -> 1.81 us  [on_device(): pl.pallas_call(finish, out_shape=(jax.ShapeDtypeStruct((GROUPS, rows, col...]
where the time goes in v2:
time: 44.4 us; the launch traced here: 44.3 us
  Pallas kernels  43.6 us (98%)
  between operations  0.64 us (1%)
    pallas_call x1, Pallas kernels, on_device(): pl.pallas_call(body, out_shape=(jax.ShapeDtypeStruct((GROUPS, rows, cols)...  41.8 us
    pallas_call x1, Pallas kernels, on_device(): pl.pallas_call(finish, out_shape=(jax.ShapeDtypeStruct((GROUPS, rows, col...  1.81 us

profile of v2, /device:TPU:1, one launch (start us, length us, event | category | flops | bytes accessed | tf_op | source)
XLA Modules:
  0.0 44.3 jit_solution(4553975480527772993)
XLA Ops:
  0.6 41.8 %litho.1 = (f32[3,128,128]{2,1,0:T(8,128)}, f32[2,128,128]{2,1,0:T(8,128)}, f32[2,128,128]{2,1,0:T(8,128)}) custom-call(s32[24]{0:T(128)} %radii_ref.1, s32[24]{0:T(128)} %group_ref.1, f32[24]{0:T(128)} %weight_ref.1, f32[24,2,128,128]{3,2,1,0:T(8,128)} %taps_hbm.1, f32[2,128,128]{2,1,0:T(8,128)} %mask_hbm.1, s32[128,128]{1,0:T(8,128)} %target_hbm.1, ...), custom_call_target="tpu_custom_call" | custom-call | tf_op jit(solution)/shard_map/litho/pallas_call | solution.py:375
  42.4 1.8 %finish.1 = (f32[3,128,128]{2,1,0:T(8,128)}, f32[2,128,128]{2,1,0:T(8,128)}) custom-call(f32[3,128,128]{2,1,0:T(8,128)} %get-tuple-element.5.power_ref, f32[2,128,128]{2,1,0:T(8,128)} %get-tuple-element.6.own_ref, f32[2,128,128]{2,1,0:T(8,128)} %get-tuple-element.7.rim_ref), custom_call_target="tpu_custom_call" | custom-call | tf_op jit(solution)/shard_map/finish/pallas_call | solution.py:407
